TPU v7x, 32 devices: a whole 2x2x4 slice. The times are simulated.
32 devices in a mesh: dp: 8 (over y, x, core), tensor: 4 (over z).
Axes of the slice: x: 2, y: 2, z: 4, core: 2. Of those that a mesh axis runs over, the one named last changes fastest.
Arguments:
- wq_flat: bfloat16 [8192, 4096], P(('dp', 'tensor')), may hold values from -0.125 to 0.125
- hidden: bfloat16 [4, 16, 8192], P(None, 'dp'), may hold values from -6 to 6
- cache: bfloat16 [16, 4, 8192, 256], P('dp', None, 'tensor'), may hold values from -300 to 300
- new_kv: bfloat16 [4, 16, 4, 256], P(None, 'dp'), may hold values from -6 to 6
- lengths: int32 [16], P('dp'), may hold values from 1 to 8192, as said below
Outputs:
- attended: bfloat16 [4, 16, 4096], P(None, 'dp', 'tensor')
Inputs may be any that keep to these rules, and one draw needn't show every extreme that they name: `lengths`: every sequence has at least one cached position; in every draw some sequence has exactly 8192.
All inputs are finite; a program needn't handle non-finite values.
Results may differ from a plain program's by a relative error of at most 0.03.
Values may be sent and summed in bfloat16 or wider, within the bound.
A program may use at most 64 MiB of HBM per device.

v0:
```python
import jax
import jax.numpy as jnp
from jax import lax
from jax.sharding import PartitionSpec as P

QH = 32
HD = 128


def merged(shard, axis, combine):
    everything = jax.tree.map(lambda part: lax.all_gather(part, axis), shard)
    initial = jax.tree.map(lambda part: part[0], everything)

    def step(k, so_far):
        return combine(so_far, jax.tree.map(lambda part: part[k], everything))

    return lax.fori_loop(1, lax.axis_size(axis), step, initial)


def combine_parts(first, second):
    best = jnp.maximum(first[0], second[0])
    scale_one = jnp.exp(first[0] - best)
    scale_two = jnp.exp(second[0] - best)
    total = first[1] * scale_one + second[1] * scale_two
    accum = first[2] * scale_one[..., None] + second[2] * scale_two[..., None]
    return (best, total, accum)


def body(wq_flat, hidden, cache, new_kv, lengths):
    n_tensor = lax.axis_size("tensor")
    n_replica = lax.axis_size("dp")
    rank = lax.axis_index("tensor")
    steps, seq_dev, width = hidden.shape
    kv_heads = cache.shape[1]
    ctx_dev = cache.shape[2]
    group = QH // kv_heads
    heads_dev = QH // n_tensor
    scale = 1.0 / HD**0.5
    rows = steps * seq_dev
    flat_rows = hidden.reshape(rows, width)
    shard_rows = wq_flat.shape[0]
    blocks = flat_rows.reshape(rows, n_replica, n_tensor, shard_rows)
    picked = lax.dynamic_index_in_dim(blocks, rank, 2, keepdims=False).reshape(
        rows, n_replica * shard_rows
    )
    partial_value = jnp.dot(
        picked,
        lax.all_gather(wq_flat, "dp", axis=0, tiled=True),
        preferred_element_type=jnp.float32,
    )
    query_all = lax.psum(partial_value, "tensor").astype(jnp.bfloat16)
    query_own = lax.dynamic_slice_in_dim(query_all, rank * heads_dev * HD, heads_dev * HD, 1)
    queries = query_all.reshape(steps, seq_dev, kv_heads, group, HD)
    keys = cache[..., :HD]
    values = cache[..., HD:]
    scores = (
        jnp.einsum("tsgjd,sgcd->gjtsc", queries, keys, preferred_element_type=jnp.float32) * scale
    )
    positions = rank * ctx_dev + jnp.arange(ctx_dev)
    valid = (positions[None, :] < lengths[:, None])[None, None, None, :, :]
    masked = jnp.where(valid, scores, -1e30)
    local_max = jnp.max(masked, axis=-1)
    weights = jnp.where(valid, jnp.exp(masked - local_max[..., None]), 0.0)
    local_total = jnp.sum(weights, axis=-1)
    local_acc = jnp.einsum(
        "gjtsc,sgcd->gjtsd",
        weights.astype(jnp.bfloat16),
        values,
        preferred_element_type=jnp.float32,
    )
    local_max = local_max.reshape(QH, steps, seq_dev)
    local_total = local_total.reshape(QH, steps, seq_dev)
    local_acc = local_acc.reshape(QH, steps, seq_dev, HD)
    best, denom, accum = merged((local_max, local_total, local_acc), "tensor", combine_parts)
    best = lax.dynamic_slice_in_dim(best, rank * heads_dev, heads_dev, 0)
    denom = lax.dynamic_slice_in_dim(denom, rank * heads_dev, heads_dev, 0)
    accum = lax.dynamic_slice_in_dim(accum, rank * heads_dev, heads_dev, 0)
    kv_index = rank * heads_dev // group
    fresh = lax.dynamic_slice_in_dim(new_kv, kv_index, 1, 2)[:, :, 0, :]
    own_q = query_own.reshape(steps, seq_dev, heads_dev, HD)
    new_scores = (
        jnp.einsum("tsjd,usd->jtsu", own_q, fresh[..., :HD], preferred_element_type=jnp.float32)
        * scale
    )
    causal = (jnp.arange(steps)[:, None] >= jnp.arange(steps)[None, :])[None, :, None, :]
    new_masked = jnp.where(causal, new_scores, -1e30)
    top = jnp.maximum(best, jnp.max(new_masked, axis=-1))
    old_scale = jnp.exp(best - top)
    new_weights = jnp.where(causal, jnp.exp(new_masked - top[..., None]), 0.0)
    denom = denom * old_scale + jnp.sum(new_weights, axis=-1)
    accum = accum * old_scale[..., None] + jnp.einsum(
        "jtsu,usd->jtsd",
        new_weights.astype(jnp.bfloat16),
        fresh[..., HD:],
        preferred_element_type=jnp.float32,
    )
    result = accum / denom[..., None]
    return result.transpose(1, 2, 0, 3).reshape(steps, seq_dev, heads_dev * HD).astype(jnp.bfloat16)


def solution(mesh):
    placed = (
        P(("dp", "tensor"), None),
        P(None, "dp", None),
        P("dp", None, "tensor", None),
        P(None, "dp", None, None),
        P("dp"),
    )
    return jax.shard_map(
        body, mesh=mesh, in_specs=placed, out_specs=P(None, "dp", "tensor"), check_vma=False
    )
```

profile of v0, /device:TPU:0, one launch (start us, length us, event | category | flops | bytes accessed | tf_op | source)
XLA Modules:
  0.0 189.2 jit_solution(12184188657150206391)
XLA Ops:
  6.5 0.0 copy-start
  6.5 0.0 copy-start.2
  6.5 0.0 copy-start.3
  6.5 0.0 all-gather.2.cloned.1.call-start
  6.5 0.7 all-gather.2.cloned.1.call-update
  7.3 0.2 copy-done.2
  7.5 0.1 reshape_reshape.3
  7.6 0.2 dynamic-slice_reduce_fusion
  7.8 0.0 copy-done
  7.9 0.0 copy-done.3
  7.9 0.1 broadcast_compare_fusion
  8.0 5.8 %fusion.34 = (bf16[2,4,2048,128]{3,2,1,0:T(8,128)(2,1)}, bf16[2,4,2048,128]{3,2,1,0:T(8,128)(2,1)}) fusion(bf16[2,4,2048,256]{3,2,1,0:T(8,128)(2,1)} %param.9), kind=kLoop, calls=%fused_computation.61 | loop fusion | bytes 16777216 | tf_op jit(solution)/shard_map/slice | solution.py:55
  13.7 88.0 %all-gather.2.cloned.1.call-done = bf16[2048,4096]{1,0:T(8,128)(2,1)} async-done(((bf16[256,4096]{1,0:T(8,128)(2,1)}), bf16[2048,4096]{1,0:T(8,128)(2,1)}) %all-gather.2.cloned.1.call-update) | async-done | bytes 16777232 | tf_op jit(solution)/shard_map/all_gather | solution.py:48
  101.7 8.0 %fusion.37 = f32[8,4096]{1,0:T(8,128)S(1)} fusion(bf16[8,2048]{1,0:T(8,128)(2,1)S(1)} %bitcast.110, bf16[2048,4096]{1,0:T(8,128)(2,1)} %all-gather.2.cloned.1.call-done), kind=kOutput, calls=%fused_computation.64 | convolution fusion | flops 134217728 | bytes 16941056 | tf_op jit(solution)/shard_map/dot_general | solution.py:46
  109.7 21.2 %all-reduce.1 = bf16[8,4096]{1,0:T(8,128)(2,1)S(1)} all-reduce(f32[8,4096]{1,0:T(8,128)S(1)} %fusion.37), channel_id=1, replica_groups=mesh['dp'=8,'tensor'=4] {'tensor'}, use_global_device_ids=true, to_apply=%region_0.1 | all-reduce | flops 32768 | bytes 196608 | tf_op jit(solution)/shard_map/psum | solution.py:51
  130.9 0.0 copy-start.1
  130.9 3.9 %fusion.35 = (f32[4,8,4,2]{1,2,3,0:T(4,128)S(1)}, f32[4,8,4,2,2048]{4,1,2,3,0:T(8,128)S(1)}) fusion(bf16[2,4,2048,128]{3,2,1,0:T(8,128)(2,1)} %get-tuple-element.230, bf16[4,2,4,8,128]{4,3,2,1,0:T(8,128)(2,1)S(1)} %bitcast.109, pred[2,2048]{1,0:T(4,128)(4,1)S(1)} %broadcast_compare_fusion), kind=kOutput, calls=%fused_computation.62 | convolution fusion | flops 135790336 | bytes 6362112 | tf_op jit(solution)/shard_map/tsgjd,sgcd->gjtsc/dot_general | solution.py:57
  134.9 0.5 fusion.11
  135.4 0.0 copy-done.1
  135.4 0.8 fusion.12
  136.2 14.7 %all_gather.15 = f32[4,32,4,2,128]{4,1,3,2,0:T(8,128)S(1)} all-gather(f32[1,32,4,2,128]{4,1,3,2,0:T(8,128)S(1)} %bitcast.107), channel_id=1, replica_groups=mesh['dp'=8,'tensor'=4] {'tensor'}, dimensions={0}, use_global_device_ids=true | all-gather | bytes 655360 | tf_op jit(solution)/shard_map/all_gather | solution.py:11
  150.9 0.1 copy.67
  151.0 0.1 reshape.67
  151.1 13.2 %all_gather.14 = f32[4,32,4,2]{1,2,3,0:T(4,128)S(1)} all-gather(f32[1,32,4,2]{1,2,3,0:T(4,128)S(1)} %reshape.67), channel_id=1, replica_groups=mesh['dp'=8,'tensor'=4] {'tensor'}, dimensions={0}, use_global_device_ids=true | all-gather | bytes 5120 | tf_op jit(solution)/shard_map/all_gather | solution.py:11
  164.3 0.1 all_gather_reshape.9
  164.4 13.2 %all_gather.13 = f32[4,32,4,2]{1,2,3,0:T(4,128)S(1)} all-gather(f32[1,32,4,2]{1,2,3,0:T(4,128)S(1)} %all_gather_reshape.9), channel_id=1, replica_groups=mesh['dp'=8,'tensor'=4] {'tensor'}, dimensions={0}, use_global_device_ids=true | all-gather | bytes 5120 | tf_op jit(solution)/shard_map/all_gather | solution.py:11
  177.6 3.3 %while.19 = (s32[]{:T(128)}, f32[32,4,2]{0,2,1:T(2,128)S(1)}, f32[32,4,2]{0,2,1:T(2,128)S(1)}, f32[32,4,2,128]{3,2,1,0:T(2,128)S(1)}, f32[4,32,4,2]{1,2,3,0:T(4,...) while((s32[]{:T(128)}, f32[32,4,2]{0,2,1:T(2,128)S(1)}, ...), condition=%wide.region_4.5_spmd, body=%wide.region_3.4_spmd.sunk | while | flops 99845 | bytes 673943 | solution.py:17
  177.7 0.1 copy.141
  177.8 0.1 copy.142
  177.9 0.8 fusion.43
  178.8 0.1 copy.141
  178.9 0.1 copy.142
  179.0 0.8 fusion.43
  179.9 0.1 copy.141
  180.0 0.1 copy.142
  180.1 0.8 fusion.43
  181.0 0.2 fusion.36
  181.2 0.1 dynamic-slice_maximum_fusion
  181.3 0.1 fusion.25
  181.4 0.1 multiply_add_fusion
  181.5 0.3 fusion.16
  181.8 0.6 copy.76
  (29 shorter events, 0.3 us)
Async XLA Ops:
  6.5 1.3 copy-start
  6.5 0.9 copy-start.2
  6.5 1.3 copy-start.3
  6.5 95.2 %all-gather.2.cloned.1.call-start = ((), (), s32[]{:S(2)}) async-start(), calls=%async_computation | async-start | bytes 18874368 | tf_op jit(solution)/shard_map/all_gather | solution.py:48
  130.9 4.4 %copy-start.1 = (bf16[2,4,2048,128]{3,2,1,0:T(8,128)(2,1)S(1)}, bf16[2,4,2048,128]{3,2,1,0:T(8,128)(2,1)}, u32[]{:S(2)}) copy-start(bf16[2,4,2048,128]{3,2,1,0:T(8,128)(2,1)} %get-tuple-element.229) | copy-start | bytes 12582916
Sparse Core Ops, SparseCore 0:
  9.2 92.4 all-gather.1
where the time goes:
time: 189 us
  waiting for transfers between devices  88.7 us (47%)
  blocking collectives  62.2 us (33%)
  between operations  13.6 us (7%)
  matrix products  13.2 us (7%)
  local copies, waits for them, and re-layouts  8.06 us (4%)
  other arithmetic  3.33 us (2%)
    all_gather x1, waiting for transfers between devices, body(): lax.all_gather(wq_flat, 'dp', axis=0, tiled=True)  88 us
    all_gather x3, blocking collectives, merged(): everything = jax.tree.map(lambda part: lax.all_gather(part, axis), shard)  41.1 us
    psum x1, blocking collectives, body(): query_all = lax.psum(partial_value, 'tensor').astype(jnp.bfloat16)  21.2 us
    dot_general x1, matrix products, body(): jnp.dot(picked, lax.all_gather(wq_flat, 'dp', axis=0, tiled=True), prefer...  8.04 us
    slice x1, local copies, waits for them, and re-layouts, body(): values = cache[..., HD:]  5.76 us
    dot_general x1, matrix products, body(): jnp.einsum('tsgjd,sgcd->gjtsc', queries, keys, preferred_element_type=jnp...  3.89 us
  transfers between devices with their start and end apart: 1, of which 1 were waited for; matrix products, arithmetic and copies ran while one was open for 3% of the time, Pallas kernels for 0%

commit v1 on v0

--- a/solution.py
+++ b/solution.py
@@ -5,6 +5,12 @@
 
 QH = 32
 HD = 128
+
+
+def summed_here(x, name):
+    parts = lax.all_gather(x, name, axis=0, tiled=False)
+    total = parts.sum(axis=0)
+    return total
 
 
 def merged(shard, axis, combine):
@@ -48,7 +54,7 @@
         lax.all_gather(wq_flat, "dp", axis=0, tiled=True),
         preferred_element_type=jnp.float32,
     )
-    query_all = lax.psum(partial_value, "tensor").astype(jnp.bfloat16)
+    query_all = summed_here(partial_value, "tensor").astype(jnp.bfloat16)
     query_own = lax.dynamic_slice_in_dim(query_all, rank * heads_dev * HD, heads_dev * HD, 1)
     queries = query_all.reshape(steps, seq_dev, kv_heads, group, HD)
     keys = cache[..., :HD]

time: 189 us -> 184 us (0.974)
  blocking collectives: 62.2 us -> 58.5 us
  matrix products: 13.2 us -> 11 us
    psum x1 -> x0, blocking collectives: 21.2 us -> none  [body(): query_all = lax.psum(partial_value, 'tensor').astype(jnp.bfloat16)]
    all_gather x0 -> x1, blocking collectives: none -> 16 us  [summed_here(): parts = lax.all_gather(x, name, axis=0, tiled=False)]
    dot_general x1, matrix products: 3.89 us -> 1.55 us  [body(): jnp.einsum('tsgjd,sgcd->gjtsc', queries, keys, preferred_element_type=jnp...]
where the time goes in v1:
time: 184 us; the launch traced here: 183 us
  waiting for transfers between devices  88.7 us (48%)
  blocking collectives  58.5 us (32%)
  between operations  13.6 us (7%)
  matrix products  11 us (6%)
  local copies, waits for them, and re-layouts  8.15 us (4%)
  other arithmetic  3.36 us (2%)
    all_gather x1, waiting for transfers between devices, body(): lax.all_gather(wq_flat, 'dp', axis=0, tiled=True)  88 us
    all_gather x3, blocking collectives, merged(): everything = jax.tree.map(lambda part: lax.all_gather(part, axis), shard)  42.5 us
    all_gather x1, blocking collectives, summed_here(): parts = lax.all_gather(x, name, axis=0, tiled=False)  16 us
    dot_general x1, matrix products, body(): jnp.dot(picked, lax.all_gather(wq_flat, 'dp', axis=0, tiled=True), prefer...  8.19 us
    slice x1, local copies, waits for them, and re-layouts, body(): values = cache[..., HD:]  5.76 us
  transfers between devices with their start and end apart: 1, of which 1 were waited for; matrix products, arithmetic and copies ran while one was open for 3% of the time, Pallas kernels for 0%

profile of v1, /device:TPU:0, one launch (start us, length us, event | category | flops | bytes accessed | tf_op | source)
XLA Modules:
  0.0 183.4 jit_solution(15900646164038380893)
XLA Ops:
  6.5 0.0 copy-start
  6.5 0.0 copy-start.3
  6.5 0.0 copy-start.4
  6.5 0.0 all-gather.3.cloned.1.call-start
  6.5 0.7 all-gather.3.cloned.1.call-update
  7.3 0.2 copy-done.3
  7.5 0.1 reshape_reshape.3
  7.6 0.2 dynamic-slice_reduce_fusion
  7.8 0.0 copy-done
  7.9 0.0 copy-done.4
  7.9 0.1 broadcast_compare_fusion
  8.0 5.8 %fusion.34 = (bf16[2,4,2048,128]{3,2,1,0:T(8,128)(2,1)}, bf16[2,4,2048,128]{3,2,1,0:T(8,128)(2,1)}) fusion(bf16[2,4,2048,256]{3,2,1,0:T(8,128)(2,1)} %param.9), kind=kLoop, calls=%fused_computation.62 | loop fusion | bytes 16777216 | tf_op jit(solution)/shard_map/slice | solution.py:61
  13.7 88.0 %all-gather.3.cloned.1.call-done = bf16[2048,4096]{1,0:T(8,128)(2,1)} async-done(((bf16[256,4096]{1,0:T(8,128)(2,1)}), bf16[2048,4096]{1,0:T(8,128)(2,1)}) %all-gather.3.cloned.1.call-update) | async-done | bytes 16777232 | tf_op jit(solution)/shard_map/all_gather | solution.py:54
  101.7 0.0 copy-start.1
  101.7 8.2 %fusion.37 = f32[8,4096]{1,0:T(8,128)S(1)} fusion(bf16[8,2048]{1,0:T(8,128)(2,1)S(1)} %bitcast.112, bf16[2048,4096]{1,0:T(8,128)(2,1)} %all-gather.3.cloned.1.call-done), kind=kOutput, calls=%fused_computation.65 | convolution fusion | flops 134217728 | bytes 16941056 | tf_op jit(solution)/shard_map/dot_general | solution.py:52
  109.9 16.0 %all-gather = f32[32,4096]{1,0:T(8,128)S(1)} all-gather(f32[8,4096]{1,0:T(8,128)S(1)} %fusion.37), channel_id=2, replica_groups=mesh['dp'=8,'tensor'=4] {'tensor'}, dimensions={0}, use_global_device_ids=true | all-gather | bytes 655360 | tf_op jit(solution)/shard_map/all_gather | solution.py:11
  126.0 0.0 copy-done.1
  126.0 0.0 copy-start.2
  126.0 1.6 fusion.35
  127.6 0.5 fusion.11
  128.1 0.1 copy-done.2
  128.2 0.8 fusion.12
  129.0 16.1 %all_gather.23 = f32[4,32,4,2,128]{4,1,3,2,0:T(8,128)S(1)} all-gather(f32[1,32,4,2,128]{4,1,3,2,0:T(8,128)S(1)} %bitcast.109), channel_id=1, replica_groups=mesh['dp'=8,'tensor'=4] {'tensor'}, dimensions={0}, use_global_device_ids=true | all-gather | bytes 655360 | tf_op jit(solution)/shard_map/all_gather | solution.py:17
  145.1 0.1 copy.66
  145.2 0.1 reshape.67
  145.3 13.2 %all_gather.22 = f32[4,32,4,2]{1,2,3,0:T(4,128)S(1)} all-gather(f32[1,32,4,2]{1,2,3,0:T(4,128)S(1)} %reshape.67), channel_id=1, replica_groups=mesh['dp'=8,'tensor'=4] {'tensor'}, dimensions={0}, use_global_device_ids=true | all-gather | bytes 5120 | tf_op jit(solution)/shard_map/all_gather | solution.py:17
  158.5 0.1 all_gather_reshape.9
  158.6 13.2 %all_gather.21 = f32[4,32,4,2]{1,2,3,0:T(4,128)S(1)} all-gather(f32[1,32,4,2]{1,2,3,0:T(4,128)S(1)} %all_gather_reshape.9), channel_id=1, replica_groups=mesh['dp'=8,'tensor'=4] {'tensor'}, dimensions={0}, use_global_device_ids=true | all-gather | bytes 5120 | tf_op jit(solution)/shard_map/all_gather | solution.py:17
  171.8 3.3 %while.19 = (s32[]{:T(128)}, f32[32,4,2]{0,2,1:T(2,128)S(1)}, f32[32,4,2]{0,2,1:T(2,128)S(1)}, f32[32,4,2,128]{3,2,1,0:T(2,128)S(1)}, f32[4,32,4,2]{1,2,3,0:T(4,...) while((s32[]{:T(128)}, f32[32,4,2]{0,2,1:T(2,128)S(1)}, ...), condition=%wide.region_4.5_spmd, body=%wide.region_3.4_spmd.sunk | while | flops 99845 | bytes 673943 | solution.py:23
  171.9 0.1 copy.140
  172.0 0.1 copy.141
  172.1 0.8 fusion.43
  173.0 0.1 copy.140
  173.1 0.1 copy.141
  173.2 0.8 fusion.43
  174.1 0.1 copy.140
  174.2 0.1 copy.141
  174.3 0.8 fusion.43
  175.2 0.2 fusion.36
  175.4 0.1 dynamic-slice_maximum_fusion
  175.5 0.1 fusion.25
  175.6 0.1 multiply_add_fusion
  175.7 0.3 fusion.16
  176.0 0.6 copy.75
  (30 shorter events, 0.4 us)
Async XLA Ops:
  6.5 1.3 copy-start
  6.5 0.9 copy-start.3
  6.5 1.3 copy-start.4
  6.5 95.2 %all-gather.3.cloned.1.call-start = ((), (), s32[]{:S(2)}) async-start(), calls=%async_computation | async-start | bytes 18874368 | tf_op jit(solution)/shard_map/all_gather | solution.py:54
  101.7 24.3 %copy-start.1 = (bf16[2,4,2048,128]{3,2,1,0:T(8,128)(2,1)S(1)}, bf16[2,4,2048,128]{3,2,1,0:T(8,128)(2,1)}, u32[]{:S(2)}) copy-start(bf16[2,4,2048,128]{3,2,1,0:T(8,128)(2,1)} %get-tuple-element.230) | copy-start | bytes 12582916
  126.0 2.2 %copy-start.2 = (bf16[2,4,2048,128]{3,2,1,0:T(8,128)(2,1)S(1)}, bf16[2,4,2048,128]{3,2,1,0:T(8,128)(2,1)}, u32[]{:S(2)}) copy-start(bf16[2,4,2048,128]{3,2,1,0:T(8,128)(2,1)} %get-tuple-element.229) | copy-start | bytes 12582916
Sparse Core Ops, SparseCore 0:
  9.2 92.4 all-gather.2
